TPU v7x, 32 devices: a whole 2x2x4 slice. The times are simulated.
32 devices in a mesh: parts: 2 (over y), step: 4 (over z), frame: 2 (over x), head: 2 (over core).
Axes of the slice: x: 2, y: 2, z: 4, core: 2. Of those that a mesh axis runs over, the one named last changes fastest.
Arguments:
- start_noise: float32 [32, 256], P('parts', 'frame'), parts along dimension 0, may hold values from -6 to 6
- position: bfloat16 [256, 1152], P('frame'), may hold values from -6 to 6
- time_table: bfloat16 [128, 1152], replicated, may hold values from -6 to 6
- time_index: int32 [4], P('step'), may hold values from 0 to 127
- sched_index: int32 [4], P('step'), may hold values from 0 to 127
- coef_keep: float32 [128], replicated, may hold values from -0.06 to -0.01
- coef_noise: float32 [128], replicated, may hold values from 0.03 to 0.12
- w_in: bfloat16 [16, 1152], replicated, may hold values from -1.5 to 1.5
- norm_gain: float32 [1152], replicated, may hold values from 0.5 to 1.5
- w_qkv: bfloat16 [1152, 3, 1152], P('step', None, 'head'), may hold values from -4 to 4
- w_proj: bfloat16 [1152, 1152], P('step', 'head'), may hold values from -0.1875 to 0.1875
- w_final: bfloat16 [16, 1152], replicated, may hold values from -0.1875 to 0.1875
Outputs:
- trajectory: float32 [4, 32, 256], P('step', 'parts', 'frame'), parts along dimension 1
- residual_norms: float32 [8], P('parts'), parts along dimension 0
There are 2 independent parts, one for each index of `parts`. A program takes and returns all parts, laid end to end along the dimension named above; an argument that names none is the same for every part. Nothing has to cross between parts.
All inputs are finite; a program needn't handle non-finite values.
Results may differ from a plain program's by a relative error of at most 0.0044.
Values may be sent and summed in bfloat16 or wider, within the bound.
A program may use at most 64 MiB of HBM per device.

v0:
```python
import math
import jax
import jax.numpy as jnp
from jax import lax
from jax.sharding import PartitionSpec as P

HDIM = 72
ITERS = 4


def entering(value, axis, combine, identity):
    count, here = (lax.axis_size(axis), lax.axis_index(axis))
    everything = lax.all_gather(value, axis)
    start = jnp.broadcast_to(jnp.asarray(identity, value.dtype), value.shape)

    def hop(k, before):
        reached = k < here
        new = combine(before, everything[k])
        return jnp.where(reached, new, before)

    return lax.fori_loop(0, count, hop, start)


def add_terms(first, second):
    return first + second


def local(
    start_noise,
    position,
    time_table,
    time_index,
    sched_index,
    coef_keep,
    coef_noise,
    w_in,
    norm_gain,
    w_qkv,
    w_proj,
    w_final,
):
    w_qkv_all, w_proj_all = (
        lax.all_gather(w_qkv, "step", axis=0, tiled=True),
        lax.all_gather(w_proj, "step", axis=0, tiled=True),
    )
    batch_steps = time_index.shape[0]
    row_count = start_noise.shape[1]
    table_rows = time_table.shape[0]
    pick_time = (time_index[:, None] == jnp.arange(table_rows)[None, :]).astype(jnp.bfloat16)
    time_embed = jnp.dot(pick_time, time_table, preferred_element_type=jnp.float32)
    pick_sched = (sched_index[:, None] == jnp.arange(table_rows)[None, :]).astype(jnp.float32)
    keep_rate = jnp.sum(pick_sched * coef_keep[None, :], axis=1)
    noise_rate = jnp.sum(pick_sched * coef_noise[None, :], axis=1)
    heads_local = w_qkv_all.shape[2] // HDIM
    cell_count = (
        batch_steps
        * lax.axis_size("step")
        * start_noise.shape[0]
        * row_count
        * lax.axis_size("frame")
    )
    states = start_noise[None]
    drift_term = jnp.zeros_like(states)
    residual_list = []
    for iteration in range(ITERS):
        latent_bf = states.astype(jnp.bfloat16)
        hidden = (
            jnp.einsum("bcr,cd->brd", latent_bf, w_in, preferred_element_type=jnp.float32)
            + position
            + time_embed[:, None, :]
        )
        normed = (
            hidden * lax.rsqrt(jnp.mean(hidden * hidden, axis=2, keepdims=True) + 1e-06) * norm_gain
        ).astype(jnp.bfloat16)
        projected = jnp.einsum(
            "brd,dkq->brkq", normed, w_qkv_all, preferred_element_type=jnp.float32
        ).astype(jnp.bfloat16)
        queries = projected[:, :, 0].reshape(batch_steps, row_count, heads_local, HDIM)
        score_scale = 1.0 / math.sqrt(HDIM)
        keys_values = projected[:, :, 1:3]
        piece = lax.all_gather(keys_values, "frame", axis=1, tiled=True)
        top_old = jnp.full((batch_steps, heads_local, row_count), -1e30, jnp.float32)
        piece_rows = piece.shape[1]
        keys_blk = piece[:, :, 0].reshape(batch_steps, piece_rows, heads_local, HDIM)
        values_blk = piece[:, :, 1].reshape(batch_steps, piece_rows, heads_local, HDIM)
        scores = (
            jnp.einsum("bqhe,bkhe->bhqk", queries, keys_blk, preferred_element_type=jnp.float32)
            * score_scale
        )
        top_new = jnp.maximum(top_old, jnp.max(scores, axis=3))
        weights_exp = jnp.exp(scores - top_new[:, :, :, None])
        total_new = jnp.sum(weights_exp, axis=3)
        update = jnp.einsum(
            "bhqk,bkhe->bqhe",
            weights_exp.astype(jnp.bfloat16),
            values_blk,
            preferred_element_type=jnp.float32,
        )
        accum = update
        top_final, total_final, accum = (top_new, total_new, accum)
        attended = accum / jnp.transpose(total_final, (0, 2, 1))[:, :, :, None]
        attn_mixed = attended.reshape(batch_steps, row_count, heads_local * HDIM).astype(
            jnp.bfloat16
        )
        partial_value = jnp.einsum(
            "brq,dq->brd", attn_mixed, w_proj_all, preferred_element_type=jnp.float32
        )
        head_total = lax.psum(partial_value, "head")
        joined = (hidden + head_total).astype(jnp.bfloat16)
        predicted = jnp.einsum("cd,brd->bcr", w_final, joined, preferred_element_type=jnp.float32)
        drift_term = keep_rate[:, None, None] * states + noise_rate[:, None, None] * predicted
        local_incl = jnp.cumsum(drift_term, axis=0)
        local_total = local_incl[-1]
        earlier = entering(local_total, "step", add_terms, jnp.zeros_like(local_total))
        before = earlier[None] + (local_incl - drift_term)
        new_states = start_noise[None] + before
        change = new_states - states
        square_sum = jnp.sum(change * change)
        summed = lax.psum(square_sum, ("step", "frame"))
        residual_list.append(jnp.sqrt(summed / cell_count + 1e-06))
        states = new_states
    residual_norms = jnp.stack(residual_list)
    trajectory = states + drift_term
    return (trajectory, residual_norms)


def solution(mesh):
    return jax.shard_map(
        local,
        mesh=mesh,
        in_specs=(
            P("parts", "frame"),
            P("frame", None),
            P(),
            P("step"),
            P("step"),
            P(),
            P(),
            P(),
            P(),
            P("step", None, "head"),
            P("step", "head"),
            P(),
        ),
        out_specs=(P("step", "parts", "frame"), P("parts")),
        check_vma=False,
    )
```

profile of v0, /device:TPU:0, one launch (start us, length us, event | category | flops | bytes accessed | tf_op | source)
XLA Modules:
  0.0 354.4 jit_solution(680078700515391486)
XLA Ops:
  7.3 0.7 all-gather.3.cloned.1.call-update
  8.0 0.7 all-gather.5.cloned.1.call-update
  9.6 0.4 multiply_reduce_fusion.3
  10.0 86.9 %all-gather.3.cloned.1.call-done = bf16[1152,3,576]{2,0,1:T(8,128)(2,1)} async-done(((bf16[288,3,576]{2,0,1:T(8,128)(2,1)}), bf16[1152,3,576]{2,0,1:T(8,128)(2,1)}) %all-gather.3.cloned.1.call-update) | async-done | bytes 3981328 | tf_op jit(solution)/shard_map/all_gather | solution.py:43
  96.9 4.0 %fusion.4 = bf16[1,128,3,576]{1,3,2,0:T(8,128)(2,1)S(1)} fusion(bf16[1152,3,576]{2,0,1:T(8,128)(2,1)} %all-gather.3.cloned.1.call-done, f32[128,1152]{1,0:T(8,128)S(1)} %get-tuple-element.432, f32[1152]{0:T(1024)S(1)} %copy-done.6, f32[128]{0:T(128)S(1)} %add_rsqrt_fusion.3), kind=kOutput, calls=%fused_computation.24 | convolution fusion | flops 510271488 | bytes 5018624 | tf_op jit(solution)/shard_map/brd,dkq->brkq/dot_general | solution.py:75
  101.0 9.3 %all_gather.31 = bf16[1,256,2,576]{1,3,2,0:T(8,128)(2,1)S(1)} all-gather(bf16[1,128,2,576]{1,3,2,0:T(8,128)(2,1)S(1)} %slice.64), channel_id=1, replica_groups=mesh['parts'=2,'step'=4,'frame'=2,'head'=2] {'frame'}, dimensions={1}, use_global_device_ids=true | all-gather | bytes 884736 | tf_op jit(solution)/shard_map/all_gather | solution.py:81
  110.3 0.4 fusion.92
  110.8 0.4 fusion.24
  111.2 0.4 fusion.17
  111.6 20.7 %all-gather.5.cloned.1.call-done = bf16[1152,576]{1,0:T(8,128)(2,1)} async-done(((bf16[288,576]{1,0:T(8,128)(2,1)}), bf16[1152,576]{1,0:T(8,128)(2,1)}) %all-gather.5.cloned.1.call-update) | async-done | bytes 1327120 | tf_op jit(solution)/shard_map/all_gather | solution.py:44
  132.3 2.8 convolution_bitcast_fusion.3
  135.8 0.6 fusion.84
  136.5 16.4 %all-reduce.6.cloned.1.call-done = f32[1,128,1152]{2,1,0:T(8,128)} async-done(((f32[1,128,1152]{2,1,0:T(8,128)}), f32[1,128,1152]{2,1,0:T(8,128)}) %all-reduce.6.cloned.1.call-update) | async-done | bytes 589840 | tf_op jit(solution)/shard_map/psum | solution.py:108
  152.9 2.5 fusion.15
  155.4 13.5 %all_gather.33 = f32[4,16,128]{2,1,0:T(8,128)S(1)} all-gather(f32[1,16,128]{2,1,0:T(8,128)S(1)} %fusion.15), channel_id=1, replica_groups=mesh['parts'=2,'step'=4,'frame'=2,'head'=2] {'step'}, dimensions={0}, use_global_device_ids=true | all-gather | bytes 40960 | tf_op jit(solution)/shard_map/all_gather | solution.py:13
  169.4 4.0 %fusion.5 = bf16[1,128,3,576]{1,3,2,0:T(8,128)(2,1)S(1)} fusion(bf16[1152,3,576]{2,0,1:T(8,128)(2,1)} %all-gather.3.cloned.1.call-done, f32[128,1152]{1,0:T(8,128)S(1)} %get-tuple-element.436, f32[128]{0:T(128)S(1)} %add_rsqrt_fusion.2, f32[1152]{0:T(1024)S(1)} %copy-done.6), kind=kOutput, calls=%fused_computation.25 | convolution fusion | flops 510271488 | bytes 5018624 | tf_op jit(solution)/shard_map/brd,dkq->brkq/dot_general | solution.py:75
  173.5 7.4 %all_gather.34 = bf16[1,256,2,576]{1,3,2,0:T(8,128)(2,1)S(1)} all-gather(bf16[1,128,2,576]{1,3,2,0:T(8,128)(2,1)S(1)} %slice.68), channel_id=1, replica_groups=mesh['parts'=2,'step'=4,'frame'=2,'head'=2] {'frame'}, dimensions={1}, use_global_device_ids=true | all-gather | bytes 884736 | tf_op jit(solution)/shard_map/all_gather | solution.py:81
  180.9 0.4 fusion.93
  181.4 0.4 fusion.26
  181.8 0.4 fusion.19
  182.2 0.6 copy-done.1
  182.8 1.4 convolution_bitcast_fusion.2
  184.3 19.7 %all-reduce.8.cloned.1.call-done = f32[1,128,1152]{2,1,0:T(8,128)} async-done(((f32[1,128,1152]{2,1,0:T(8,128)}), f32[1,128,1152]{2,1,0:T(8,128)}) %all-reduce.8.cloned.1.call-update) | async-done | bytes 589840 | tf_op jit(solution)/shard_map/psum | solution.py:108
  203.9 2.5 fusion.13
  206.4 13.5 %all_gather.35 = f32[4,16,128]{2,1,0:T(8,128)S(1)} all-gather(f32[1,16,128]{2,1,0:T(8,128)S(1)} %fusion.13), channel_id=1, replica_groups=mesh['parts'=2,'step'=4,'frame'=2,'head'=2] {'step'}, dimensions={0}, use_global_device_ids=true | all-gather | bytes 40960 | tf_op jit(solution)/shard_map/all_gather | solution.py:13
  220.1 0.4 multiply_reduce_fusion.1
  220.4 4.0 %fusion.6 = bf16[1,128,3,576]{1,3,2,0:T(8,128)(2,1)S(1)} fusion(bf16[1152,3,576]{2,0,1:T(8,128)(2,1)} %all-gather.3.cloned.1.call-done, f32[128,1152]{1,0:T(8,128)S(1)} %get-tuple-element.440, f32[128]{0:T(128)S(1)} %add_rsqrt_fusion.1, f32[1152]{0:T(1024)S(1)} %copy-done.6), kind=kOutput, calls=%fused_computation.26 | convolution fusion | flops 510271488 | bytes 5018624 | tf_op jit(solution)/shard_map/brd,dkq->brkq/dot_general | solution.py:75
  224.5 7.4 %all_gather.36 = bf16[1,256,2,576]{1,3,2,0:T(8,128)(2,1)S(1)} all-gather(bf16[1,128,2,576]{1,3,2,0:T(8,128)(2,1)S(1)} %slice.72), channel_id=1, replica_groups=mesh['parts'=2,'step'=4,'frame'=2,'head'=2] {'frame'}, dimensions={1}, use_global_device_ids=true | all-gather | bytes 884736 | tf_op jit(solution)/shard_map/all_gather | solution.py:81
  232.0 0.4 fusion.94
  232.4 0.4 fusion.28
  232.8 0.4 fusion.21
  233.2 1.4 convolution_bitcast_fusion.1
  234.9 19.5 %all-reduce.10.cloned.1.call-done = f32[1,128,1152]{2,1,0:T(8,128)} async-done(((f32[1,128,1152]{2,1,0:T(8,128)}), f32[1,128,1152]{2,1,0:T(8,128)}) %all-reduce.10.cloned.1.call-update) | async-done | bytes 589840 | tf_op jit(solution)/shard_map/psum | solution.py:108
  254.4 2.5 fusion.11
  256.9 13.5 %all_gather.37 = f32[4,16,128]{2,1,0:T(8,128)S(1)} all-gather(f32[1,16,128]{2,1,0:T(8,128)S(1)} %fusion.11), channel_id=1, replica_groups=mesh['parts'=2,'step'=4,'frame'=2,'head'=2] {'step'}, dimensions={0}, use_global_device_ids=true | all-gather | bytes 40960 | tf_op jit(solution)/shard_map/all_gather | solution.py:13
  270.5 0.4 multiply_reduce_fusion
  270.9 4.0 %fusion.7 = bf16[1,128,3,576]{1,3,2,0:T(8,128)(2,1)S(1)} fusion(bf16[1152,3,576]{2,0,1:T(8,128)(2,1)} %all-gather.3.cloned.1.call-done, f32[128,1152]{1,0:T(8,128)S(1)} %get-tuple-element.444, f32[128]{0:T(128)S(1)} %add_rsqrt_fusion, f32[1152]{0:T(1024)S(1)} %copy-done.6), kind=kOutput, calls=%fused_computation.27 | convolution fusion | flops 510271488 | bytes 5018624 | tf_op jit(solution)/shard_map/brd,dkq->brkq/dot_general | solution.py:75
  275.0 7.4 %all_gather.38 = bf16[1,256,2,576]{1,3,2,0:T(8,128)(2,1)S(1)} all-gather(bf16[1,128,2,576]{1,3,2,0:T(8,128)(2,1)S(1)} %slice.76), channel_id=1, replica_groups=mesh['parts'=2,'step'=4,'frame'=2,'head'=2] {'frame'}, dimensions={1}, use_global_device_ids=true | all-gather | bytes 884736 | tf_op jit(solution)/shard_map/all_gather | solution.py:81
  282.5 0.4 fusion.95
  282.9 0.4 fusion.30
  283.3 0.4 fusion.23
  283.7 1.4 convolution_bitcast_fusion
  285.1 19.7 %all-reduce.12.cloned.1.call-done = f32[1,128,1152]{2,1,0:T(8,128)} async-done(((f32[1,128,1152]{2,1,0:T(8,128)}), f32[1,128,1152]{2,1,0:T(8,128)}) %all-reduce.12.cloned.1.call-update) | async-done | bytes 589840 | tf_op jit(solution)/shard_map/psum | solution.py:108
  304.9 2.5 fusion.9
  307.3 13.5 %all_gather.39 = f32[4,16,128]{2,1,0:T(8,128)S(1)} all-gather(f32[1,16,128]{2,1,0:T(8,128)S(1)} %fusion.9), channel_id=1, replica_groups=mesh['parts'=2,'step'=4,'frame'=2,'head'=2] {'step'}, dimensions={0}, use_global_device_ids=true | all-gather | bytes 40960 | tf_op jit(solution)/shard_map/all_gather | solution.py:13
  321.0 1.3 fusion.73
  322.2 22.0 %all-reduce = (f32[]{:T(128)}, f32[]{:T(128)}, f32[]{:T(128)}, f32[]{:T(128)}) all-reduce(f32[]{:T(128)} %get-tuple-element.383, f32[]{:T(128)} %get-tuple-element.384, f32[]{:T(128)} %get-tuple-element.385, f32[]{:T(128)} %get-tuple-element.382), channel_id=1, replica_groups=mesh['parts'=2,'step'=4,'frame'=2,'head'=2] {'step','frame'}, use_global_device_ids=true, to_apply=%region_33.34 | all-reduce | flops 4 | bytes 32 | tf_op jit(solution)/shard_map/psum | solution.py:119
  347.0 0.6 pad_maximum_fusion
  (76 shorter events, 1.9 us)
Async XLA Ops:
  7.2 2.2 copy-start
  7.2 2.4 copy-start.5
  7.2 2.4 copy-start.2
  7.2 2.4 copy-start.3
  7.2 89.7 %copy-start.6 = (f32[1152]{0:T(1024)S(1)}, f32[1152]{0:T(1024)}, u32[]{:S(2)}) copy-start(f32[1152]{0:T(1024)} %param.28) | copy-start | bytes 13828
  7.2 89.7 %all-gather.3.cloned.1.call-start = ((), (), s32[]{:S(2)}) async-start(), calls=%async_computation | async-start | bytes 5529600 | tf_op jit(solution)/shard_map/all_gather | solution.py:43
  8.0 124.3 %all-gather.5.cloned.1.call-start = ((), (), s32[]{:S(2)}) async-start(), calls=%async_computation.1 | async-start | bytes 1843200 | tf_op jit(solution)/shard_map/all_gather | solution.py:44
  8.7 144.2 %all-reduce.6.cloned.1.call-start = ((), (), s32[]{:S(2)}) async-start(), calls=%async_computation.2 | async-start | bytes 1179648 | tf_op jit(solution)/shard_map/psum | solution.py:108
  111.6 24.2 %copy-start.7 = (f32[128]{0:T(128)S(1)}, f32[128]{0:T(128)}, u32[]{:S(2)}) copy-start(f32[128]{0:T(128)} %param.25) | copy-start | bytes 1540
  111.6 24.2 %copy-start.8 = (f32[128]{0:T(128)S(1)}, f32[128]{0:T(128)}, u32[]{:S(2)}) copy-start(f32[128]{0:T(128)} %param.26) | copy-start | bytes 1540
  111.6 41.3 %copy-start.4 = (bf16[16,1152]{1,0:T(8,128)(2,1)S(1)}, bf16[16,1152]{1,0:T(8,128)(2,1)}, u32[]{:S(2)}) copy-start(bf16[16,1152]{1,0:T(8,128)(2,1)} %param.31) | copy-start | bytes 110596
  135.1 68.9 %all-reduce.8.cloned.1.call-start = ((), (), s32[]{:S(2)}) async-start(), calls=%async_computation.3 | async-start | bytes 1179648 | tf_op jit(solution)/shard_map/psum | solution.py:108
  181.4 1.4 copy-start.1
  184.2 70.2 %all-reduce.10.cloned.1.call-start = ((), (), s32[]{:S(2)}) async-start(), calls=%async_computation.4 | async-start | bytes 1179648 | tf_op jit(solution)/shard_map/psum | solution.py:108
  234.7 70.2 %all-reduce.12.cloned.1.call-start = ((), (), s32[]{:S(2)}) async-start(), calls=%async_computation.5 | async-start | bytes 1179648 | tf_op jit(solution)/shard_map/psum | solution.py:108
Sparse Core Ops, SparseCore 0:
  9.6 87.2 all-gather.2
  98.4 33.7 all-gather.4
  135.2 17.6 all-reduce.5
  184.3 19.5 all-reduce.7
  234.8 19.5 all-reduce.9
  285.2 19.5 all-reduce.11
where the time goes:
time: 355 us; the launch traced here: 354 us
  waiting for transfers between devices  184 us (52%)
  blocking collectives  108 us (30%)
  matrix products  38 us (11%)
  between operations  18.5 us (5%)
  other arithmetic  4.24 us (1%)
    all_gather x1, waiting for transfers between devices, local(): lax.all_gather(w_qkv, 'step', axis=0, tiled=True)  86.9 us
    psum x4, waiting for transfers between devices, local(): head_total = lax.psum(partial_value, 'head')  75.4 us
    all_gather x4, blocking collectives, entering(): everything = lax.all_gather(value, axis)  54.1 us
    all_gather x4, blocking collectives, local(): piece = lax.all_gather(keys_values, 'frame', axis=1, tiled=True)  31.6 us
    psum x1, blocking collectives, local(): summed = lax.psum(square_sum, ('step', 'frame'))  22 us
    all_gather x1, waiting for transfers between devices, local(): lax.all_gather(w_proj, 'step', axis=0, tiled=True)  20.7 us
    dot_general x4, matrix products, local(): jnp.einsum('brd,dkq->brkq', normed, w_qkv_all, preferred_element_type=jnp...  16.1 us
    dot_general x4, matrix products, local(): jnp.einsum('cd,brd->bcr', w_final, joined, preferred_element_type=jnp.flo...  9.96 us
  transfers between devices with their start and end apart: 6, of which 6 were waited for; matrix products, arithmetic and copies ran while one was open for 2% of the time, Pallas kernels for 0%

commit v1 on v0

--- a/solution.py
+++ b/solution.py
@@ -105,7 +105,7 @@
         partial_value = jnp.einsum(
             "brq,dq->brd", attn_mixed, w_proj_all, preferred_element_type=jnp.float32
         )
-        head_total = lax.psum(partial_value, "head")
+        head_total = jnp.sum(lax.all_gather(partial_value, "head"), axis=0)
         joined = (hidden + head_total).astype(jnp.bfloat16)
         predicted = jnp.einsum("cd,brd->bcr", w_final, joined, preferred_element_type=jnp.float32)
         drift_term = keep_rate[:, None, None] * states + noise_rate[:, None, None] * predicted

time: 355 us -> 319 us (0.90)
  waiting for transfers between devices: 184 us -> 146 us
  other arithmetic: 4.24 us -> 10.5 us
  matrix products: 38 us -> 33.7 us
    psum x4 -> x0, waiting for transfers between devices: 75.4 us -> none  [local(): head_total = lax.psum(partial_value, 'head')]
    all_gather x0 -> x4, waiting for transfers between devices: none -> 37 us  [local(): head_total = jnp.sum(lax.all_gather(partial_value, 'head'), axis=0)]
    reduce_sum x0 -> x5, other arithmetic: none -> 6.26 us  [the longest x4 5.61 us: local(): head_total = jnp.sum(lax.all_gather(partial_value, 'head'), axis=0)]
    dot_general x4, matrix products: 9.96 us -> 5.67 us  [local(): jnp.einsum('cd,brd->bcr', w_final, joined, preferred_element_type=jnp.flo...]
where the time goes in v1:
time: 319 us; the launch traced here: 318 us
  waiting for transfers between devices  146 us (46%)
  blocking collectives  108 us (34%)
  matrix products  33.7 us (11%)
  between operations  18.5 us (6%)
  other arithmetic  10.5 us (3%)
    all_gather x1, waiting for transfers between devices, local(): lax.all_gather(w_qkv, 'step', axis=0, tiled=True)  86.9 us
    all_gather x4, blocking collectives, entering(): everything = lax.all_gather(value, axis)  53.9 us
    all_gather x4, waiting for transfers between devices, local(): head_total = jnp.sum(lax.all_gather(partial_value, 'head'), axis=0)  37 us
    all_gather x4, blocking collectives, local(): piece = lax.all_gather(keys_values, 'frame', axis=1, tiled=True)  31.8 us
    psum x1, blocking collectives, local(): summed = lax.psum(square_sum, ('step', 'frame'))  22 us
    all_gather x1, waiting for transfers between devices, local(): lax.all_gather(w_proj, 'step', axis=0, tiled=True)  20.7 us
    dot_general x4, matrix products, local(): jnp.einsum('brd,dkq->brkq', normed, w_qkv_all, preferred_element_type=jnp...  16.1 us
    dot_general x4, matrix products, local(): jnp.einsum('brq,dq->brd', attn_mixed, w_proj_all, preferred_element_type=...  7.05 us
  transfers between devices with their start and end apart: 6, of which 6 were waited for; matrix products, arithmetic and copies ran while one was open for 2% of the time, Pallas kernels for 0%

profile of v1, /device:TPU:0, one launch (start us, length us, event | category | flops | bytes accessed | tf_op | source)
XLA Modules:
  0.0 317.9 jit_solution(2549496247262070554)
XLA Ops:
  7.3 0.7 all-gather.11.cloned.1.call-update
  8.0 0.7 all-gather.13.cloned.1.call-update
  10.0 86.9 %all-gather.11.cloned.1.call-done = bf16[1152,3,576]{2,0,1:T(8,128)(2,1)} async-done(((bf16[288,3,576]{2,0,1:T(8,128)(2,1)}), bf16[1152,3,576]{2,0,1:T(8,128)(2,1)}) %all-gather.11.cloned.1.call-update) | async-done | bytes 3981328 | tf_op jit(solution)/shard_map/all_gather | solution.py:43
  96.9 4.0 %fusion.4 = bf16[1,128,3,576]{1,3,2,0:T(8,128)(2,1)S(1)} fusion(bf16[1152,3,576]{2,0,1:T(8,128)(2,1)} %all-gather.11.cloned.1.call-done, f32[128,1152]{1,0:T(8,128)S(1)} %get-tuple-element.432, f32[1152]{0:T(1024)S(1)} %copy-done.6, f32[128]{0:T(128)S(1)} %add_rsqrt_fusion.3), kind=kOutput, calls=%fused_computation.20 | convolution fusion | flops 510271488 | bytes 5018624 | tf_op jit(solution)/shard_map/brd,dkq->brkq/dot_general | solution.py:75
  100.9 9.3 %all_gather.55 = bf16[1,256,2,576]{1,3,2,0:T(8,128)(2,1)S(1)} all-gather(bf16[1,128,2,576]{1,3,2,0:T(8,128)(2,1)S(1)} %slice.64), channel_id=1, replica_groups=mesh['parts'=2,'step'=4,'frame'=2,'head'=2] {'frame'}, dimensions={1}, use_global_device_ids=true | all-gather | bytes 884736 | tf_op jit(solution)/shard_map/all_gather | solution.py:81
  110.3 0.4 fusion.80
  110.8 0.4 fusion.24
  111.1 0.4 fusion.17
  111.6 20.7 %all-gather.13.cloned.1.call-done = bf16[1152,576]{1,0:T(8,128)(2,1)} async-done(((bf16[288,576]{1,0:T(8,128)(2,1)}), bf16[1152,576]{1,0:T(8,128)(2,1)}) %all-gather.13.cloned.1.call-update) | async-done | bytes 1327120 | tf_op jit(solution)/shard_map/all_gather | solution.py:44
  132.3 2.8 fusion.84
  135.8 0.6 fusion.72
  136.4 0.7 fusion.73
  137.1 6.3 %all-gather.15.cloned.1.call-done = f32[256,1152]{1,0:T(8,128)} async-done(((f32[128,1152]{1,0:T(8,128)}), f32[256,1152]{1,0:T(8,128)}) %all-gather.15.cloned.1.call-update) | async-done | bytes 1179664 | tf_op jit(solution)/shard_map/all_gather | solution.py:108
  143.4 1.4 reduce.32
  144.8 1.4 fusion.15
  146.2 13.5 %all_gather.59 = f32[4,16,128]{2,1,0:T(8,128)S(1)} all-gather(f32[1,16,128]{2,1,0:T(8,128)S(1)} %fusion.15), channel_id=1, replica_groups=mesh['parts'=2,'step'=4,'frame'=2,'head'=2] {'step'}, dimensions={0}, use_global_device_ids=true | all-gather | bytes 40960 | tf_op jit(solution)/shard_map/all_gather | solution.py:13
  160.2 4.0 %fusion.5 = bf16[1,128,3,576]{1,3,2,0:T(8,128)(2,1)S(1)} fusion(bf16[1152,3,576]{2,0,1:T(8,128)(2,1)} %all-gather.11.cloned.1.call-done, f32[128,1152]{1,0:T(8,128)S(1)} %get-tuple-element.436, f32[128]{0:T(128)S(1)} %add_rsqrt_fusion.2, f32[1152]{0:T(1024)S(1)} %copy-done.6), kind=kOutput, calls=%fused_computation.21 | convolution fusion | flops 510271488 | bytes 5018624 | tf_op jit(solution)/shard_map/brd,dkq->brkq/dot_general | solution.py:75
  164.3 7.4 %all_gather.60 = bf16[1,256,2,576]{1,3,2,0:T(8,128)(2,1)S(1)} all-gather(bf16[1,128,2,576]{1,3,2,0:T(8,128)(2,1)S(1)} %slice.68), channel_id=1, replica_groups=mesh['parts'=2,'step'=4,'frame'=2,'head'=2] {'frame'}, dimensions={1}, use_global_device_ids=true | all-gather | bytes 884736 | tf_op jit(solution)/shard_map/all_gather | solution.py:81
  171.7 0.4 fusion.81
  172.6 0.4 fusion.19
  173.0 0.6 copy-done.1
  173.5 1.4 fusion.85
  175.0 10.2 %all-gather.17.cloned.1.call-done = f32[256,1152]{1,0:T(8,128)} async-done(((f32[128,1152]{1,0:T(8,128)}), f32[256,1152]{1,0:T(8,128)}) %all-gather.17.cloned.1.call-update) | async-done | bytes 1179664 | tf_op jit(solution)/shard_map/all_gather | solution.py:108
  185.3 1.4 reduce.33
  186.7 1.4 fusion.13
  188.1 13.5 %all_gather.63 = f32[4,16,128]{2,1,0:T(8,128)S(1)} all-gather(f32[1,16,128]{2,1,0:T(8,128)S(1)} %fusion.13), channel_id=1, replica_groups=mesh['parts'=2,'step'=4,'frame'=2,'head'=2] {'step'}, dimensions={0}, use_global_device_ids=true | all-gather | bytes 40960 | tf_op jit(solution)/shard_map/all_gather | solution.py:13
  202.1 4.0 %fusion.6 = bf16[1,128,3,576]{1,3,2,0:T(8,128)(2,1)S(1)} fusion(bf16[1152,3,576]{2,0,1:T(8,128)(2,1)} %all-gather.11.cloned.1.call-done, f32[128,1152]{1,0:T(8,128)S(1)} %get-tuple-element.440, f32[128]{0:T(128)S(1)} %add_rsqrt_fusion.1, f32[1152]{0:T(1024)S(1)} %copy-done.6), kind=kOutput, calls=%fused_computation.22 | convolution fusion | flops 510271488 | bytes 5018624 | tf_op jit(solution)/shard_map/brd,dkq->brkq/dot_general | solution.py:75
  206.1 7.6 %all_gather.64 = bf16[1,256,2,576]{1,3,2,0:T(8,128)(2,1)S(1)} all-gather(bf16[1,128,2,576]{1,3,2,0:T(8,128)(2,1)S(1)} %slice.72), channel_id=1, replica_groups=mesh['parts'=2,'step'=4,'frame'=2,'head'=2] {'frame'}, dimensions={1}, use_global_device_ids=true | all-gather | bytes 884736 | tf_op jit(solution)/shard_map/all_gather | solution.py:81
  213.8 0.4 fusion.82
  214.6 0.4 fusion.21
  215.0 1.4 fusion.86
  216.5 10.2 %all-gather.19.cloned.1.call-done = f32[256,1152]{1,0:T(8,128)} async-done(((f32[128,1152]{1,0:T(8,128)}), f32[256,1152]{1,0:T(8,128)}) %all-gather.19.cloned.1.call-update) | async-done | bytes 1179664 | tf_op jit(solution)/shard_map/all_gather | solution.py:108
  226.7 1.4 reduce.34
  228.1 1.4 fusion.11
  229.5 13.5 %all_gather.67 = f32[4,16,128]{2,1,0:T(8,128)S(1)} all-gather(f32[1,16,128]{2,1,0:T(8,128)S(1)} %fusion.11), channel_id=1, replica_groups=mesh['parts'=2,'step'=4,'frame'=2,'head'=2] {'step'}, dimensions={0}, use_global_device_ids=true | all-gather | bytes 40960 | tf_op jit(solution)/shard_map/all_gather | solution.py:13
  243.5 4.0 %fusion.7 = bf16[1,128,3,576]{1,3,2,0:T(8,128)(2,1)S(1)} fusion(bf16[1152,3,576]{2,0,1:T(8,128)(2,1)} %all-gather.11.cloned.1.call-done, f32[128,1152]{1,0:T(8,128)S(1)} %get-tuple-element.444, f32[128]{0:T(128)S(1)} %add_rsqrt_fusion, f32[1152]{0:T(1024)S(1)} %copy-done.6), kind=kOutput, calls=%fused_computation.23 | convolution fusion | flops 510271488 | bytes 5018624 | tf_op jit(solution)/shard_map/brd,dkq->brkq/dot_general | solution.py:75
  247.6 7.4 %all_gather.68 = bf16[1,256,2,576]{1,3,2,0:T(8,128)(2,1)S(1)} all-gather(bf16[1,128,2,576]{1,3,2,0:T(8,128)(2,1)S(1)} %slice.76), channel_id=1, replica_groups=mesh['parts'=2,'step'=4,'frame'=2,'head'=2] {'frame'}, dimensions={1}, use_global_device_ids=true | all-gather | bytes 884736 | tf_op jit(solution)/shard_map/all_gather | solution.py:81
  255.0 0.4 fusion.83
  255.5 0.4 fusion.30
  255.9 0.4 fusion.23
  256.3 1.4 fusion.87
  257.7 10.3 %all-gather.21.cloned.1.call-done = f32[256,1152]{1,0:T(8,128)} async-done(((f32[128,1152]{1,0:T(8,128)}), f32[256,1152]{1,0:T(8,128)}) %all-gather.21.cloned.1.call-update) | async-done | bytes 1179664 | tf_op jit(solution)/shard_map/all_gather | solution.py:108
  268.0 1.4 reduce.35
  269.4 1.4 fusion.9
  270.8 13.5 %all_gather.71 = f32[4,16,128]{2,1,0:T(8,128)S(1)} all-gather(f32[1,16,128]{2,1,0:T(8,128)S(1)} %fusion.9), channel_id=1, replica_groups=mesh['parts'=2,'step'=4,'frame'=2,'head'=2] {'step'}, dimensions={0}, use_global_device_ids=true | all-gather | bytes 40960 | tf_op jit(solution)/shard_map/all_gather | solution.py:13
  284.4 1.3 fusion.61
  285.7 22.0 %all-reduce = (f32[]{:T(128)}, f32[]{:T(128)}, f32[]{:T(128)}, f32[]{:T(128)}) all-reduce(f32[]{:T(128)} %get-tuple-element.383, f32[]{:T(128)} %get-tuple-element.384, f32[]{:T(128)} %get-tuple-element.385, f32[]{:T(128)} %get-tuple-element.382), channel_id=1, replica_groups=mesh['parts'=2,'step'=4,'frame'=2,'head'=2] {'step','frame'}, use_global_device_ids=true, to_apply=%region_33.34 | all-reduce | flops 4 | bytes 32 | tf_op jit(solution)/shard_map/psum | solution.py:119
  310.4 0.6 pad_maximum_fusion
  (81 shorter events, 3.6 us)
Async XLA Ops:
  7.2 2.2 copy-start
  7.2 2.4 copy-start.5
  7.2 2.4 copy-start.2
  7.2 2.4 copy-start.3
  7.2 89.7 %copy-start.6 = (f32[1152]{0:T(1024)S(1)}, f32[1152]{0:T(1024)}, u32[]{:S(2)}) copy-start(f32[1152]{0:T(1024)} %param.28) | copy-start | bytes 13828
  7.2 89.7 %all-gather.11.cloned.1.call-start = ((), (), s32[]{:S(2)}) async-start(), calls=%async_computation | async-start | bytes 5529600 | tf_op jit(solution)/shard_map/all_gather | solution.py:43
  8.0 124.3 %all-gather.13.cloned.1.call-start = ((), (), s32[]{:S(2)}) async-start(), calls=%async_computation.1 | async-start | bytes 1843200 | tf_op jit(solution)/shard_map/all_gather | solution.py:44
  8.7 134.7 %all-gather.15.cloned.1.call-start = ((), (), s32[]{:S(2)}) async-start(), calls=%async_computation.2 | async-start | bytes 1769472 | tf_op jit(solution)/shard_map/all_gather | solution.py:108
  111.5 24.2 %copy-start.7 = (f32[128]{0:T(128)S(1)}, f32[128]{0:T(128)}, u32[]{:S(2)}) copy-start(f32[128]{0:T(128)} %param.25) | copy-start | bytes 1540
  111.5 24.9 %copy-start.8 = (f32[128]{0:T(128)S(1)}, f32[128]{0:T(128)}, u32[]{:S(2)}) copy-start(f32[128]{0:T(128)} %param.26) | copy-start | bytes 1540
  135.0 9.8 %copy-start.4 = (bf16[16,1152]{1,0:T(8,128)(2,1)S(1)}, bf16[16,1152]{1,0:T(8,128)(2,1)}, u32[]{:S(2)}) copy-start(bf16[16,1152]{1,0:T(8,128)(2,1)} %param.31) | copy-start | bytes 110596
  135.1 50.2 %all-gather.17.cloned.1.call-start = ((), (), s32[]{:S(2)}) async-start(), calls=%async_computation.3 | async-start | bytes 1769472 | tf_op jit(solution)/shard_map/all_gather | solution.py:108
  172.2 1.4 copy-start.1
  175.0 51.7 %all-gather.19.cloned.1.call-start = ((), (), s32[]{:S(2)}) async-start(), calls=%async_computation.4 | async-start | bytes 1769472 | tf_op jit(solution)/shard_map/all_gather | solution.py:108
  216.4 51.6 %all-gather.21.cloned.1.call-start = ((), (), s32[]{:S(2)}) async-start(), calls=%async_computation.5 | async-start | bytes 1769472 | tf_op jit(solution)/shard_map/all_gather | solution.py:108
Sparse Core Ops, SparseCore 0:
  9.6 87.2 all-gather.10
  98.4 33.7 all-gather.12
  135.2 8.1 all-gather.14
  175.1 10.1 all-gather.16
  216.6 10.0 all-gather.18
  257.9 10.0 all-gather.20
